TPU v7x, 32 devices: a whole 2x2x4 slice. The times are simulated.
32 devices in a mesh: tm: 2 (over x), seq: 16 (over z, y, core).
Axes of the slice: x: 2, y: 2, z: 4, core: 2. Of those that a mesh axis runs over, the one named last changes fastest.
Arguments:
- tokens: bfloat16 [512, 5120], P(('tm', 'seq')), may hold values from -6 to 6
- w_query: bfloat16 [5120, 4096], P('seq'), may hold values from -0.078125 to 0.078125
- w_out: bfloat16 [4096, 5120], P(None, 'seq'), may hold values from -0.25 to 0.25
- k_cache: bfloat16 [4096, 4096], P(('tm', 'seq')), may hold values from -800 to 800
- v_cache: bfloat16 [4096, 4096], P(('tm', 'seq')), may hold values from -6 to 6
- radial_mask: int32 [16, 2, 32], replicated, may hold values from 0 to 1, as said below
- slot_frame: int32 [16], replicated, may hold values from 0 to 15, each once
Outputs:
- mixed: bfloat16 [512, 5120], P(('tm', 'seq'))
Inputs may be any that keep to these rules, and one draw needn't show every extreme that they name: radial_mask[f, b, f * 2 + b] = 1 for every frame f and tile b. `slot_frame`: each of the 16 frames is held by exactly one slot.
All inputs are finite; a program needn't handle non-finite values.
Results may differ from a plain program's by a relative error of at most 0.012.
The roundings to bfloat16 on the way count: a program that leaves them out, or rounds other values in their place, can miss the bound.
Values may be sent and summed in bfloat16 or wider, within the bound.
A program may use at most 128 MiB of HBM per device.

v0:
```python
import jax
import jax.numpy as jnp
from jax import lax
from jax.sharding import PartitionSpec as P

D = 5120
HD = 128
HEADS = 32
FRAMES = 16
BLOCK = 128
Q_DEV = 16
NEG = -1e30


def spread_columns(table, blocks, copies, groups):
    rows = table.shape[0]
    head_width = table.shape[1] // blocks
    grouped = table.reshape(rows, 1, blocks, 1, head_width)
    spread = jnp.broadcast_to(grouped, (rows, groups, blocks, copies, head_width))
    return spread.reshape(rows, groups * blocks * copies, head_width)


def on_device(tokens, w_query, w_out, k_cache, v_cache, radial_mask, slot_frame):
    seq_count = lax.axis_size("seq")
    group_count = lax.axis_size("tm")
    copies = max(1, seq_count // HEADS)
    per_dev = HEADS * copies // seq_count
    head_width = per_dev * HD
    blocks = seq_count // copies
    part_rows = Q_DEV // copies
    query_rows = part_rows * seq_count
    frame_tok = Q_DEV * seq_count
    frame_blocks = frame_tok // BLOCK
    per_group = FRAMES // group_count
    key_tile = 4 * BLOCK
    score_scale = HD ** (-0.5)
    my_seq = lax.axis_index("seq")
    my_group = lax.axis_index("tm")
    my_part = my_seq % copies
    split_rows = (
        tokens.reshape(copies, part_rows, D).transpose(1, 0, 2).reshape(part_rows, 1, copies, D)
    )
    token_send = jnp.broadcast_to(split_rows, (part_rows, blocks, copies, D)).reshape(
        part_rows, seq_count, D
    )
    query_send = spread_columns(w_query, blocks, copies, 1)
    frame = lax.dynamic_index_in_dim(slot_frame, my_group * per_group, 0, keepdims=False)
    onehot = (slot_frame[:, None] == lax.iota(jnp.int32, FRAMES)[None, :]).astype(jnp.float32)
    chosen = lax.dynamic_index_in_dim(radial_mask, frame, 0, keepdims=False).astype(jnp.float32)
    chosen = chosen.reshape(frame_blocks, FRAMES, frame_blocks)
    mask_slots = jnp.einsum("sf,qfb->qsb", onehot, chosen).reshape(
        frame_blocks, FRAMES * frame_blocks
    )
    row_index = lax.iota(jnp.int32, query_rows)
    token_index = row_index // part_rows * Q_DEV + my_part * part_rows + row_index % part_rows
    row_block = (token_index // BLOCK)[:, None] == lax.iota(jnp.int32, frame_blocks)[None, :]
    row_allowed = jnp.dot(
        row_block.astype(jnp.float32), mask_slots, preferred_element_type=jnp.float32
    )
    key_send = spread_columns(k_cache, blocks, copies, 1)
    value_send = spread_columns(v_cache, blocks, copies, 1)
    token_got, query_got, key_got, value_got = (
        lax.all_to_all(token_send, "seq", split_axis=1, concat_axis=0, tiled=True),
        lax.all_to_all(query_send, "seq", split_axis=1, concat_axis=0, tiled=True),
        lax.all_to_all(key_send, "seq", split_axis=1, concat_axis=0, tiled=True),
        lax.all_to_all(value_send, "seq", split_axis=1, concat_axis=0, tiled=True),
    )
    query = jnp.dot(
        token_got.reshape(query_rows, D),
        query_got.reshape(D, head_width),
        preferred_element_type=jnp.float32,
    )
    query = query.astype(jnp.bfloat16).reshape(query_rows, per_dev, HD)
    start_state = (
        jnp.full((query_rows, per_dev), NEG, jnp.float32),
        jnp.zeros((query_rows, per_dev), jnp.float32),
        jnp.zeros((query_rows, per_dev, HD), jnp.float32),
    )
    group_keys = key_got.reshape(-1, head_width)
    group_values = value_got.reshape(-1, head_width)
    keys = lax.all_gather(group_keys, "tm", axis=0, tiled=True)
    values = lax.all_gather(group_values, "tm", axis=0, tiled=True)
    tiles = keys.shape[0] // key_tile

    def one_tile(index, state):
        highest, denom, summed = state
        k_tile = lax.dynamic_slice_in_dim(keys, index * key_tile, key_tile, 0).reshape(
            key_tile, per_dev, HD
        )
        v_tile = lax.dynamic_slice_in_dim(values, index * key_tile, key_tile, 0).reshape(
            key_tile, per_dev, HD
        )
        first_block = index * key_tile // BLOCK
        allowed = lax.dynamic_slice_in_dim(row_allowed, first_block, key_tile // BLOCK, 1)
        keep = jnp.repeat(allowed > 0.5, BLOCK, axis=1)[:, None, :]
        scores = (
            jnp.einsum("qhd,khd->qhk", query, k_tile, preferred_element_type=jnp.float32)
            * score_scale
        )
        scores = jnp.where(keep, scores, NEG)
        new_high = jnp.maximum(highest, jnp.max(scores, axis=2))
        weights = jnp.where(keep, jnp.exp(scores - new_high[..., None]), 0.0)
        fade = jnp.exp(highest - new_high)
        denom = denom * fade + jnp.sum(weights, axis=2)
        update = jnp.einsum(
            "qhk,khd->qhd", weights.astype(jnp.bfloat16), v_tile, preferred_element_type=jnp.float32
        )
        summed = summed * fade[..., None] + update
        return (new_high, denom, summed)

    final_state = lax.fori_loop(0, tiles, one_tile, start_state)
    attended = (
        (final_state[2] / final_state[1][..., None])
        .astype(jnp.bfloat16)
        .reshape(query_rows, head_width)
    )
    out_columns = w_out.shape[1]
    every_head = lax.all_gather(attended[None], "seq", axis=0, tiled=True)
    every_head = every_head.reshape(blocks, copies, seq_count, part_rows, head_width)
    w_blocks = w_out.reshape(blocks, head_width, out_columns)
    columns = jnp.einsum(
        "bcsrw,bwo->scro", every_head, w_blocks, preferred_element_type=jnp.float32
    )
    columns = columns.reshape(frame_tok, out_columns).astype(jnp.bfloat16)
    mixed = lax.all_to_all(columns, "seq", split_axis=0, concat_axis=1, tiled=True)
    return mixed


def solution(mesh):
    return jax.shard_map(
        on_device,
        mesh=mesh,
        in_specs=(
            P(("tm", "seq"), None),
            P("seq", None),
            P(None, "seq"),
            P(("tm", "seq"), None),
            P(("tm", "seq"), None),
            P(),
            P(),
        ),
        out_specs=P(("tm", "seq"), None),
        check_vma=False,
    )
```

profile of v0, /device:TPU:0, one launch (start us, length us, event | category | flops | bytes accessed | tf_op | source)
XLA Modules:
  0.0 300.3 jit_solution(17684607203295914071)
XLA Ops:
  6.5 2.4 copy.52
  8.9 7.4 %all-to-all-start = ((bf16[128,16,256]{0,2,1:T(8,128)(2,1)}), bf16[128,16,256]{0,2,1:T(8,128)(2,1)S(1)}, u32[]{:S(2)}, u32[]{:S(2)}) async-start(bf16[128,16,256]{0,2,1:T(8,128)(2,1)} %bitcast.3), calls=%async_computation | async-start | bytes 2097152 | tf_op jit(solution)/shard_map/all_to_all | solution.py:65
  16.3 1.3 copy.55
  17.6 21.6 %all-to-all-done = bf16[128,16,256]{0,2,1:T(8,128)(2,1)S(1)} async-done(((bf16[128,16,256]{0,2,1:T(8,128)(2,1)}), bf16[128,16,256]{0,2,1:T(8,128)(2,1)S(1)}, u32[]{:S(2)}, u32[]{:S(2)}) %all-to-all-start) | async-done | bytes 1048608 | tf_op jit(solution)/shard_map/all_to_all | solution.py:65
  40.2 6.8 %all-to-all-start.3 = ((bf16[128,16,256]{0,2,1:T(8,128)(2,1)}), bf16[128,16,256]{0,2,1:T(8,128)(2,1)S(1)}, u32[]{:S(2)}, u32[]{:S(2)}) async-start(bf16[128,16,256]{0,2,1:T(8,128)(2,1)} %bitcast.14), calls=%async_computation.3 | async-start | bytes 2097152 | tf_op jit(solution)/shard_map/all_to_all | solution.py:66
  47.0 3.5 %copy.81 = bf16[40,16,8,256]{3,2,0,1:T(8,128)(2,1)} copy(bf16[40,16,8,256]{3,2,1,0:T(8,128)(2,1)} %bitcast.88) | data formatting | bytes 5242880 | tf_op jit(solution)/shard_map/reshape;reshape | solution.py:20
  50.5 19.4 %all-to-all-done.3 = bf16[128,16,256]{0,2,1:T(8,128)(2,1)S(1)} async-done(((bf16[128,16,256]{0,2,1:T(8,128)(2,1)}), bf16[128,16,256]{0,2,1:T(8,128)(2,1)S(1)}, u32[]{:S(2)}, u32[]{:S(2)}) %all-to-all-start.3) | async-done | bytes 1048608 | tf_op jit(solution)/shard_map/all_to_all | solution.py:66
  70.9 65.3 %all_to_all.76 = bf16[320,16,256]{2,0,1:T(8,128)(2,1)S(1)} all-to-all(bf16[320,16,256]{2,0,1:T(8,128)(2,1)} %bitcast.85), channel_id=1, replica_groups=mesh['tm'=2,'seq'=16] {'seq'}, dimensions={1} | all-to-all | bytes 5242880 | tf_op jit(solution)/shard_map/all_to_all | solution.py:64
  136.2 1.8 reshape.112
  138.1 5.2 %all-to-all-start.1 = ((bf16[16,16,5120]{2,0,1:T(8,128)(2,1)}), bf16[16,16,5120]{2,0,1:T(8,128)(2,1)}, u32[]{:S(2)}, u32[]{:S(2)}) async-start(bf16[16,16,5120]{2,0,1:T(8,128)(2,1)} %reshape.112), calls=%async_computation.1 | async-start | bytes 5242880 | tf_op jit(solution)/shard_map/all_to_all | solution.py:63
  143.4 2.3 copy.53
  145.7 2.3 copy.56
  151.9 41.6 %all-to-all-done.1 = bf16[16,16,5120]{2,0,1:T(8,128)(2,1)} async-done(((bf16[16,16,5120]{2,0,1:T(8,128)(2,1)}), bf16[16,16,5120]{2,0,1:T(8,128)(2,1)}, u32[]{:S(2)}, u32[]{:S(2)}) %all-to-all-start.1) | async-done | bytes 2621472 | tf_op jit(solution)/shard_map/all_to_all | solution.py:63
  193.5 2.9 convolution_convert_fusion
  196.5 18.4 %all-gather.6.cloned.1.call-done = bf16[4096,256]{1,0:T(8,128)(2,1)} async-done(((bf16[2048,256]{1,0:T(8,128)(2,1)}), bf16[4096,256]{1,0:T(8,128)(2,1)}) %all-gather.6.cloned.1.call-update) | async-done | bytes 2097168 | tf_op jit(solution)/shard_map/all_gather | solution.py:82
  214.9 20.1 %while.20 = (s32[]{:T(128)}, f32[256,2]{0,1:T(2,128)S(1)}, f32[256,2]{0,1:T(2,128)S(1)}, f32[256,2,128]{0,2,1:T(8,128)S(1)}, f32[256,32]{0,1:T(8,128)S(1)}, /*in...) while((s32[]{:T(128)}, f32[256,2]{0,1:T(2,128)S(1)}, ...), condition=%wide.region_3.4_spmd.clone, body=%wide.region_0.3_spmd.clone.sunk | while | flops 136777248 | bytes 6986118 | solution.py:111
  214.9 1.1 constant_dynamic-slice_fusion.3
  219.9 1.1 constant_dynamic-slice_fusion.3
  225.0 1.1 constant_dynamic-slice_fusion.3
  227.5 1.1 constant_dynamic-slice_fusion.3
  235.8 2.6 copy.73
  238.3 39.0 %all-gather.8.cloned.1.call-done = bf16[16,256,256]{2,1,0:T(8,128)(2,1)} async-done(((bf16[1,256,256]{2,1,0:T(8,128)(2,1)}), bf16[16,256,256]{2,1,0:T(8,128)(2,1)}) %all-gather.8.cloned.1.call-update) | async-done | bytes 2097168 | tf_op jit(solution)/shard_map/all_gather | solution.py:118
  277.4 3.3 %fusion.17 = bf16[16,16,320]{2,1,0:T(8,128)(2,1)S(1)} fusion(bf16[16,16,16,256]{3,2,1,0:T(8,128)(2,1)} %bitcast.94, bf16[16,256,320,1]{1,0,2,3:T(8,128)(2,1)S(1)} %bitcast.90), kind=kOutput, calls=%fused_computation.25 | convolution fusion | flops 671170560 | bytes 4882432 | tf_op jit(solution)/shard_map/bcsrw,bwo->scro/dot_general | solution.py:121
  280.7 12.2 %all_to_all.77 = bf16[16,16,320]{2,1,0:T(8,128)(2,1)S(1)} all-to-all(bf16[16,16,320]{2,1,0:T(8,128)(2,1)S(1)} %fusion.17), channel_id=1, replica_groups=mesh['tm'=2,'seq'=16] {'seq'}, dimensions={0} | all-to-all | bytes 327680 | tf_op jit(solution)/shard_map/all_to_all | solution.py:125
  (117 shorter events, 21.0 us)
Async XLA Ops:
  6.5 9.8 %copy-start.2 = (bf16[128,4096]{1,0:T(8,128)(2,1)S(1)}, bf16[128,4096]{1,0:T(8,128)(2,1)}, u32[]{:S(2)}) copy-start(bf16[128,4096]{1,0:T(8,128)(2,1)} %param.13) | copy-start | bytes 3145732
  8.9 30.3 %all-to-all-start = ((bf16[128,16,256]{0,2,1:T(8,128)(2,1)}), bf16[128,16,256]{0,2,1:T(8,128)(2,1)S(1)}, u32[]{:S(2)}, u32[]{:S(2)}) async-start(bf16[128,16,256]{0,2,1:T(8,128)(2,1)} %bitcast.3), calls=%async_computation | async-start | bytes 2097152 | tf_op jit(solution)/shard_map/all_to_all | solution.py:65
  39.2 1.0 copy-start.1
  40.2 29.7 %all-to-all-start.3 = ((bf16[128,16,256]{0,2,1:T(8,128)(2,1)}), bf16[128,16,256]{0,2,1:T(8,128)(2,1)S(1)}, u32[]{:S(2)}, u32[]{:S(2)}) async-start(bf16[128,16,256]{0,2,1:T(8,128)(2,1)} %bitcast.14), calls=%async_computation.3 | async-start | bytes 2097152 | tf_op jit(solution)/shard_map/all_to_all | solution.py:66
  69.9 1.0 copy-start
  70.9 65.3 %copy-start.3 = (bf16[16,5120]{1,0:T(8,128)(2,1)S(1)}, bf16[16,5120]{1,0:T(8,128)(2,1)}, u32[]{:S(2)}) copy-start(bf16[16,5120]{1,0:T(8,128)(2,1)} %param.9) | copy-start | bytes 491524
  138.1 55.4 %all-to-all-start.1 = ((bf16[16,16,5120]{2,0,1:T(8,128)(2,1)}), bf16[16,16,5120]{2,0,1:T(8,128)(2,1)}, u32[]{:S(2)}, u32[]{:S(2)}) async-start(bf16[16,16,5120]{2,0,1:T(8,128)(2,1)} %reshape.112), calls=%async_computation.1 | async-start | bytes 5242880 | tf_op jit(solution)/shard_map/all_to_all | solution.py:63
  143.3 53.2 %all-gather.4.cloned.1.call-start = ((), (), s32[]{:S(2)}) async-start(), calls=%async_computation.5 | async-start | bytes 3145728 | tf_op jit(solution)/shard_map/all_gather | solution.py:81
  145.6 2.4 copy-start.4
  145.7 69.2 %all-gather.6.cloned.1.call-start = ((), (), s32[]{:S(2)}) async-start(), calls=%async_computation.6 | async-start | bytes 3145728 | tf_op jit(solution)/shard_map/all_gather | solution.py:82
  148.0 129.4 %all-gather.8.cloned.1.call-start = ((), (), s32[]{:S(2)}) async-start(), calls=%async_computation.7 | async-start | bytes 2228224 | tf_op jit(solution)/shard_map/all_gather | solution.py:118
Sparse Core Ops, SparseCore 0:
  145.8 34.3 all-gather.3
  181.7 33.0 all-gather.5
  235.9 41.4 all-gather.7
where the time goes:
time: 301 us; the launch traced here: 300 us
  waiting for transfers between devices  140 us (47%)
  blocking collectives  77.5 us (26%)
  local copies, waits for them, and re-layouts  32 us (11%)
  starting transfers between devices  19.5 us (6%)
  between operations  15 us (5%)
  matrix products  12.6 us (4%)
    all_to_all x1, blocking collectives, on_device(): lax.all_to_all(query_send, 'seq', split_axis=1, concat_axis=0, tiled=True)  65.3 us
    all_to_all x1, waiting for transfers between devices, on_device(): lax.all_to_all(token_send, 'seq', split_axis=1, concat_axis=0, tiled=True)  41.6 us
    all_gather x1, waiting for transfers between devices, on_device(): every_head = lax.all_gather(attended[None], 'seq', axis=0, tiled=True)  39 us
    all_to_all x1, waiting for transfers between devices, on_device(): lax.all_to_all(key_send, 'seq', split_axis=1, concat_axis=0, tiled=True)  21.6 us
    all_to_all x1, waiting for transfers between devices, on_device(): lax.all_to_all(value_send, 'seq', split_axis=1, concat_axis=0, tiled=True)  19.4 us
    all_gather x1, waiting for transfers between devices, on_device(): values = lax.all_gather(group_values, 'tm', axis=0, tiled=True)  18.4 us
    all_to_all x1, blocking collectives, on_device(): lax.all_to_all(columns, 'seq', split_axis=0, concat_axis=1, tiled=True)  12.2 us
    dynamic_slice x16, local copies, waits for them, and re-layouts, one_tile(): lax.dynamic_slice_in_dim(values, index * key_tile, key_tile, 0)  9.69 us
  transfers between devices with their start and end apart: 6, of which 5 were waited for; matrix products, arithmetic and copies ran while one was open for 6% of the time, Pallas kernels for 0%

commit v1 on v0

--- a/solution.py
+++ b/solution.py
@@ -63,7 +63,12 @@
         lax.all_to_all(token_send, "seq", split_axis=1, concat_axis=0, tiled=True),
         lax.all_to_all(query_send, "seq", split_axis=1, concat_axis=0, tiled=True),
         lax.all_to_all(key_send, "seq", split_axis=1, concat_axis=0, tiled=True),
-        lax.all_to_all(value_send, "seq", split_axis=1, concat_axis=0, tiled=True),
+        jnp.concatenate(
+            lax.all_to_all(
+                jnp.stack(jnp.split(value_send, lax.axis_size("seq"), axis=1)), "seq", 0, 0
+            ),
+            axis=0,
+        ),
     )
     query = jnp.dot(
         token_got.reshape(query_rows, D),

time: 301 us -> 319 us (1.060)
  local copies, waits for them, and re-layouts: 32 us -> 49.1 us
    all_gather x1, waiting for transfers between devices: 0.02 us -> 18.4 us  [on_device(): keys = lax.all_gather(group_keys, 'tm', axis=0, tiled=True)]
    all_gather x1, waiting for transfers between devices: 18.4 us -> 0.02 us  [on_device(): values = lax.all_gather(group_values, 'tm', axis=0, tiled=True)]
    unnamed x14 -> x29, local copies, waits for them, and re-layouts: 8.43 us -> 17.2 us
    dynamic_slice x8 -> x16, local copies, waits for them, and re-layouts: 1.12 us -> 8.91 us  [one_tile(): lax.dynamic_slice_in_dim(keys, index * key_tile, key_tile, 0)]
    dynamic_slice x16 -> x8, local copies, waits for them, and re-layouts: 9.69 us -> 7.8 us  [one_tile(): lax.dynamic_slice_in_dim(values, index * key_tile, key_tile, 0)]
  transfers between devices with their start and end apart: 6 -> 6, of which waited for: 5 -> 5; matrix products, arithmetic and copies ran while one was open for 6% -> 5% of each run, Pallas kernels for 0% -> 0%
where the time goes in v1:
time: 319 us; the launch traced here: 318 us
  waiting for transfers between devices  140 us (44%)
  blocking collectives  77.5 us (24%)
  local copies, waits for them, and re-layouts  49.1 us (15%)
  starting transfers between devices  19.5 us (6%)
  between operations  15.1 us (5%)
  matrix products  12.6 us (4%)
    all_to_all x1, blocking collectives, on_device(): lax.all_to_all(query_send, 'seq', split_axis=1, concat_axis=0, tiled=True)  65.3 us
    all_to_all x1, waiting for transfers between devices, on_device(): lax.all_to_all(token_send, 'seq', split_axis=1, concat_axis=0, tiled=True)  41.6 us
    all_gather x1, waiting for transfers between devices, on_device(): every_head = lax.all_gather(attended[None], 'seq', axis=0, tiled=True)  39 us
    all_to_all x1, waiting for transfers between devices, on_device(): lax.all_to_all(jnp.stack(jnp.split(value_send, lax.axis_size('seq'), axis...  21.6 us
    all_to_all x1, waiting for transfers between devices, on_device(): lax.all_to_all(key_send, 'seq', split_axis=1, concat_axis=0, tiled=True)  19.4 us
    all_gather x1, waiting for transfers between devices, on_device(): keys = lax.all_gather(group_keys, 'tm', axis=0, tiled=True)  18.4 us
    unnamed x29, local copies, waits for them, and re-layouts  17.2 us
    all_to_all x1, blocking collectives, on_device(): lax.all_to_all(columns, 'seq', split_axis=0, concat_axis=1, tiled=True)  12.2 us
  transfers between devices with their start and end apart: 6, of which 5 were waited for; matrix products, arithmetic and copies ran while one was open for 5% of the time, Pallas kernels for 0%

profile of v1, /device:TPU:0, one launch (start us, length us, event | category | flops | bytes accessed | tf_op | source)
XLA Modules:
  0.0 317.5 jit_solution(10437849301972547669)
XLA Ops:
  6.5 1.6 copy.104
  20.2 7.4 %all-to-all-start.3 = ((bf16[16,128,1,256]{3,1,2,0:T(8,128)(2,1)}), bf16[16,128,1,256]{3,1,2,0:T(8,128)(2,1)S(1)}, u32[]{:S(2)}, u32[]{:S(2)}) async-start(bf16[16,128,1,256]{3,1,2,0:T(8,128)(2,1)} %bitcast_dynamic-update-slice_fusion), calls=%async_computation.3 | async-start | bytes 2097152 | tf_op jit(solution)/shard_map/all_to_all | solution.py:67
  27.6 1.3 copy.101
  28.9 21.6 %all-to-all-done.3 = bf16[16,128,1,256]{3,1,2,0:T(8,128)(2,1)S(1)} async-done(((bf16[16,128,1,256]{3,1,2,0:T(8,128)(2,1)}), bf16[16,128,1,256]{3,1,2,0:T(8,128)(2,1)S(1)}, u32[]{:S(2)}, u32[]{:S(2)}) %all-to-all-start.3) | async-done | bytes 1048608 | tf_op jit(solution)/shard_map/all_to_all | solution.py:67
  50.5 1.0 copy-done.1
  51.5 6.8 %all-to-all-start = ((bf16[128,16,256]{0,2,1:T(8,128)(2,1)}), bf16[128,16,256]{0,2,1:T(8,128)(2,1)S(1)}, u32[]{:S(2)}, u32[]{:S(2)}) async-start(bf16[128,16,256]{0,2,1:T(8,128)(2,1)} %bitcast.3), calls=%async_computation | async-start | bytes 2097152 | tf_op jit(solution)/shard_map/all_to_all | solution.py:65
  58.3 3.5 %copy.144 = bf16[40,16,8,256]{3,2,0,1:T(8,128)(2,1)} copy(bf16[40,16,8,256]{3,2,1,0:T(8,128)(2,1)} %bitcast.117) | data formatting | bytes 5242880 | tf_op jit(solution)/shard_map/reshape;reshape | solution.py:20
  61.8 19.4 %all-to-all-done = bf16[128,16,256]{0,2,1:T(8,128)(2,1)S(1)} async-done(((bf16[128,16,256]{0,2,1:T(8,128)(2,1)}), bf16[128,16,256]{0,2,1:T(8,128)(2,1)S(1)}, u32[]{:S(2)}, u32[]{:S(2)}) %all-to-all-start) | async-done | bytes 1048608 | tf_op jit(solution)/shard_map/all_to_all | solution.py:65
  81.2 1.0 copy-done
  82.2 65.3 %all_to_all.66 = bf16[320,16,256]{2,0,1:T(8,128)(2,1)S(1)} all-to-all(bf16[320,16,256]{2,0,1:T(8,128)(2,1)} %bitcast.113), channel_id=1, replica_groups=mesh['tm'=2,'seq'=16] {'seq'}, dimensions={1} | all-to-all | bytes 5242880 | tf_op jit(solution)/shard_map/all_to_all | solution.py:64
  147.6 1.8 reshape.108
  149.4 5.2 %all-to-all-start.1 = ((bf16[16,16,5120]{2,0,1:T(8,128)(2,1)}), bf16[16,16,5120]{2,0,1:T(8,128)(2,1)}, u32[]{:S(2)}, u32[]{:S(2)}) async-start(bf16[16,16,5120]{2,0,1:T(8,128)(2,1)} %reshape.108), calls=%async_computation.1 | async-start | bytes 5242880 | tf_op jit(solution)/shard_map/all_to_all | solution.py:63
  154.7 2.3 copy.121
  157.0 2.3 copy.102
  163.2 41.6 %all-to-all-done.1 = bf16[16,16,5120]{2,0,1:T(8,128)(2,1)} async-done(((bf16[16,16,5120]{2,0,1:T(8,128)(2,1)}), bf16[16,16,5120]{2,0,1:T(8,128)(2,1)}, u32[]{:S(2)}, u32[]{:S(2)}) %all-to-all-start.1) | async-done | bytes 2621472 | tf_op jit(solution)/shard_map/all_to_all | solution.py:63
  204.8 2.9 convolution_convert_fusion
  207.8 18.4 %all-gather.4.cloned.1.call-done = bf16[4096,256]{1,0:T(8,128)(2,1)} async-done(((bf16[2048,256]{1,0:T(8,128)(2,1)}), bf16[4096,256]{1,0:T(8,128)(2,1)}) %all-gather.4.cloned.1.call-update) | async-done | bytes 2097168 | tf_op jit(solution)/shard_map/all_gather | solution.py:86
  226.2 25.9 %while.20 = (s32[]{:T(128)}, f32[256,2]{0,1:T(2,128)S(1)}, f32[256,2]{0,1:T(2,128)S(1)}, f32[256,2,128]{0,2,1:T(8,128)S(1)}, f32[256,32]{0,1:T(8,128)S(1)}, /*in...) while((s32[]{:T(128)}, f32[256,2]{0,1:T(2,128)S(1)}, ...), condition=%wide.region_3.4_spmd.clone, body=%wide.region_0.3_spmd.clone.sunk | while | flops 136777248 | bytes 6461834 | solution.py:116
  228.0 1.0 constant_dynamic-slice_fusion.5
  244.2 1.0 constant_dynamic-slice_fusion.5
  252.9 2.6 copy.136
  255.5 39.0 %all-gather.8.cloned.1.call-done = bf16[16,256,256]{2,1,0:T(8,128)(2,1)} async-done(((bf16[1,256,256]{2,1,0:T(8,128)(2,1)}), bf16[16,256,256]{2,1,0:T(8,128)(2,1)}) %all-gather.8.cloned.1.call-update) | async-done | bytes 2097168 | tf_op jit(solution)/shard_map/all_gather | solution.py:123
  294.6 3.3 %fusion.17 = bf16[16,16,320]{2,1,0:T(8,128)(2,1)S(1)} fusion(bf16[16,16,16,256]{3,2,1,0:T(8,128)(2,1)} %bitcast.123, bf16[16,256,320,1]{1,0,2,3:T(8,128)(2,1)S(1)} %bitcast.119), kind=kOutput, calls=%fused_computation.25 | convolution fusion | flops 671170560 | bytes 4882432 | tf_op jit(solution)/shard_map/bcsrw,bwo->scro/dot_general | solution.py:126
  297.9 12.2 %all_to_all.67 = bf16[16,16,320]{2,1,0:T(8,128)(2,1)S(1)} all-to-all(bf16[16,16,320]{2,1,0:T(8,128)(2,1)S(1)} %fusion.17), channel_id=1, replica_groups=mesh['tm'=2,'seq'=16] {'seq'}, dimensions={0} | all-to-all | bytes 327680 | tf_op jit(solution)/shard_map/all_to_all | solution.py:130
  (150 shorter events, 39.0 us)
Async XLA Ops:
  9.7 17.9 %copy-start.2 = (bf16[128,4096]{1,0:T(8,128)(2,1)S(1)}, bf16[128,4096]{1,0:T(8,128)(2,1)}, u32[]{:S(2)}) copy-start(bf16[128,4096]{1,0:T(8,128)(2,1)} %param.12) | copy-start | bytes 3145732
  20.2 30.3 %all-to-all-start.3 = ((bf16[16,128,1,256]{3,1,2,0:T(8,128)(2,1)}), bf16[16,128,1,256]{3,1,2,0:T(8,128)(2,1)S(1)}, u32[]{:S(2)}, u32[]{:S(2)}) async-start(bf16[16,128,1,256]{3,1,2,0:T(8,128)(2,1)} %bitcast_dynamic-update-slice_fusion), calls=%async_computation.3 | async-start | bytes 2097152 | tf_op jit(solution)/shard_map/all_to_all | solution.py:67
  50.5 1.0 copy-start.1
  51.5 29.7 %all-to-all-start = ((bf16[128,16,256]{0,2,1:T(8,128)(2,1)}), bf16[128,16,256]{0,2,1:T(8,128)(2,1)S(1)}, u32[]{:S(2)}, u32[]{:S(2)}) async-start(bf16[128,16,256]{0,2,1:T(8,128)(2,1)} %bitcast.3), calls=%async_computation | async-start | bytes 2097152 | tf_op jit(solution)/shard_map/all_to_all | solution.py:65
  81.2 1.0 copy-start
  82.2 65.3 %copy-start.3 = (bf16[16,5120]{1,0:T(8,128)(2,1)S(1)}, bf16[16,5120]{1,0:T(8,128)(2,1)}, u32[]{:S(2)}) copy-start(bf16[16,5120]{1,0:T(8,128)(2,1)} %param.9) | copy-start | bytes 491524
  149.4 55.4 %all-to-all-start.1 = ((bf16[16,16,5120]{2,0,1:T(8,128)(2,1)}), bf16[16,16,5120]{2,0,1:T(8,128)(2,1)}, u32[]{:S(2)}, u32[]{:S(2)}) async-start(bf16[16,16,5120]{2,0,1:T(8,128)(2,1)} %reshape.108), calls=%async_computation.1 | async-start | bytes 5242880 | tf_op jit(solution)/shard_map/all_to_all | solution.py:63
  154.6 53.2 %all-gather.6.cloned.1.call-start = ((), (), s32[]{:S(2)}) async-start(), calls=%async_computation.6 | async-start | bytes 3145728 | tf_op jit(solution)/shard_map/all_gather | solution.py:87
  157.0 2.4 copy-start.4
  157.0 69.2 %all-gather.4.cloned.1.call-start = ((), (), s32[]{:S(2)}) async-start(), calls=%async_computation.5 | async-start | bytes 3145728 | tf_op jit(solution)/shard_map/all_gather | solution.py:86
  159.3 135.2 %all-gather.8.cloned.1.call-start = ((), (), s32[]{:S(2)}) async-start(), calls=%async_computation.7 | async-start | bytes 2228224 | tf_op jit(solution)/shard_map/all_gather | solution.py:123
Sparse Core Ops, SparseCore 0:
  157.1 34.3 all-gather.5
  193.0 33.0 all-gather.3
  253.1 41.4 all-gather.7
